TPU v7x, 32 devices: a whole 2x2x4 slice. The times are simulated.
32 devices in a mesh: grp: 2 (over x), res: 16 (over z, y, core).
Axes of the slice: x: 2, y: 2, z: 4, core: 2. Of those that a mesh axis runs over, the one named last changes fastest.
Arguments:
- stacked_sequence_embedding: bfloat16 [1024, 8192], P(('grp', 'res')), parts along dimension 0, may hold values from -6 to 6
- normalizer_multiplier: float32 [64], replicated, may hold values from 0.1 to 1.9
- normalizer_additive: float32 [64], replicated, may hold values from -2 to 2
- lhs_projected_tensor: bfloat16 [64, 32], replicated, may hold values from -0.75 to 0.75
- rhs_projected_tensor: bfloat16 [64, 32], replicated, may hold values from -0.75 to 0.75
- pairwise_matrix: bfloat16 [1024, 128], replicated, may hold values from -0.359375 to 0.359375
- pairwise_shift: float32 [128], replicated, may hold values from -3 to 3
Outputs:
- pair_update: bfloat16 [256, 128, 128], P(('grp', 'res')), parts along dimension 0
There are 2 independent parts, one for each index of `grp`. A program takes and returns all parts, laid end to end along the dimension named above; an argument that names none is the same for every part. Nothing has to cross between parts.
All inputs are finite; a program needn't handle non-finite values.
Results may differ from a plain program's by a relative error of at most 0.0047.
Values may be sent and summed in bfloat16 or wider, within the bound.
A program may use at most 128 MiB of HBM per device.

v0:
```python
import jax
import jax.numpy as jnp
from jax import lax
from jax.sharding import PartitionSpec as P


def normalize(member_list, normalizer_multiplier, normalizer_additive):
    center = member_list - jnp.mean(member_list, axis=-1, keepdims=True)
    spread = jnp.mean(center * center, axis=-1, keepdims=True)
    return (
        center * lax.rsqrt(spread + 1e-05) * normalizer_multiplier + normalizer_additive
    ).astype(jnp.bfloat16)


def project_both(
    member_list,
    normalizer_multiplier,
    normalizer_additive,
    lhs_projected_tensor,
    rhs_projected_tensor,
    rows,
    residues,
):
    chans = lhs_projected_tensor.shape[0]
    width = lhs_projected_tensor.shape[1]
    normed = normalize(
        member_list.astype(jnp.float32).reshape(rows * residues, chans),
        normalizer_multiplier,
        normalizer_additive,
    )
    left = (
        jnp.dot(normed, lhs_projected_tensor, preferred_element_type=jnp.float32)
        .astype(jnp.bfloat16)
        .reshape(rows, residues * width)
    )
    right = (
        jnp.dot(normed, rhs_projected_tensor, preferred_element_type=jnp.float32)
        .astype(jnp.bfloat16)
        .reshape(rows, residues * width)
    )
    return (left, right)


def pair_block(left, piece, pairwise_matrix, pairwise_shift, width):
    rows = left.shape[0]
    left_count = left.shape[1] // width
    right_count = piece.shape[1] // width
    outer = (
        lax.dot_general(left, piece, (((0,), (0,)), ((), ())), preferred_element_type=jnp.float32)
        / rows
    )
    flat = outer.reshape(left_count, width, right_count, width).transpose(0, 2, 1, 3)
    flat = flat.reshape(left_count * right_count, width * width).astype(jnp.bfloat16)
    mapped = jnp.dot(flat, pairwise_matrix, preferred_element_type=jnp.float32) + pairwise_shift
    return mapped.astype(jnp.bfloat16).reshape(left_count, right_count, pairwise_matrix.shape[1])


def on_device(
    stacked_sequence_embedding,
    normalizer_multiplier,
    normalizer_additive,
    lhs_projected_tensor,
    rhs_projected_tensor,
    pairwise_matrix,
    pairwise_shift,
):
    chans = lhs_projected_tensor.shape[0]
    width = lhs_projected_tensor.shape[1]
    partition_numbers = lax.all_to_all(
        stacked_sequence_embedding, "res", split_axis=1, concat_axis=0, tiled=True
    )
    rows = partition_numbers.shape[0]
    resid = partition_numbers.shape[1] // chans
    left, right = project_both(
        partition_numbers,
        normalizer_multiplier,
        normalizer_additive,
        lhs_projected_tensor,
        rhs_projected_tensor,
        rows,
        resid,
    )
    return pair_block(
        left,
        lax.all_gather(right, "res", axis=1, tiled=True),
        pairwise_matrix,
        pairwise_shift,
        width,
    )


def solution(mesh):
    in_specs = (P(("grp", "res"), None), P(), P(), P(), P(), P(), P())
    out_specs = P(("grp", "res"), None, None)
    return jax.shard_map(
        on_device, mesh=mesh, in_specs=in_specs, out_specs=out_specs, check_vma=False
    )
```

profile of v0, /device:TPU:0, one launch (start us, length us, event | category | flops | bytes accessed | tf_op | source)
XLA Modules:
  0.0 116.2 jit_solution(17071124105977982926)
XLA Ops:
  6.5 0.0 copy-start
  6.5 0.0 all-gather.2.cloned.1.call-start
  6.5 1.1 copy.23
  7.7 21.7 %all_to_all.13 = bf16[32,16,512]{2,0,1:T(8,128)(2,1)S(1)} all-to-all(bf16[32,16,512]{2,0,1:T(8,128)(2,1)S(1)} %bitcast.28), channel_id=1, replica_groups=mesh['grp'=2,'res'=16] {'res'}, dimensions={1} | all-to-all | bytes 1048576 | tf_op jit(solution)/shard_map/all_to_all | solution.py:69
  29.3 0.1 convert_bitcast_fusion
  29.5 0.4 reshape.38
  29.9 0.0 copy-start.3
  29.9 0.0 copy-start.4
  29.9 0.6 reduce_sum.18
  30.5 1.3 %multiply_reduce_fusion = f32[4096]{0:T(1024)S(1)} fusion(f32[4096,64]{1,0:T(8,128)S(1)} %reshape.38, f32[4096]{0:T(1024)S(1)} %broadcast_multiply_fusion), kind=kLoop, calls=%fused_computation.8 | loop fusion | flops 782336 | bytes 1081344 | tf_op jit(solution)/shard_map/reduce_sum | solution.py:9
  31.8 0.0 copy-start.1
  31.8 0.0 copy-done.3
  31.9 0.0 copy-done.4
  31.9 2.3 %add_convert_fusion = bf16[4096,64]{1,0:T(8,128)(2,1)S(1)} fusion(f32[4096,64]{1,0:T(8,128)S(1)} %reshape.38, f32[64]{0:T(128)S(1)} %copy-done.3, f32[64]{0:T(128)S(1)} %copy-done.4, f32[4096]{0:T(1024)S(1)} %add_rsqrt_fusion, f32[4096]{0:T(1024)S(1)} %broadcast_multiply_fusion), kind=kLoop, calls=%fused_computation.7 | loop fusion | flops 1310720 | bytes 1606144 | tf_op jit(solution)/shard_map/convert_element_type | solution.py:12
  34.2 0.0 copy-done.1
  34.2 0.0 copy-start.2
  34.2 0.4 convolution_convert_fusion
  34.6 0.5 copy.10
  35.1 1.4 %reshape.36 = bf16[512,256]{1,0:T(8,128)(2,1)} reshape(bf16[4096,32]{1,0:T(8,128)(2,1)S(1)} %copy.10) | data formatting | bytes 524288 | tf_op jit(solution)/shard_map/reshape | solution.py:39
  36.6 0.0 all-gather.2.cloned.1.call-update
  36.6 0.0 copy-done.2
  36.6 0.4 convolution_convert_fusion.1
  37.1 0.5 copy.9
  37.6 0.7 reshape.35
  38.3 51.1 %all-gather.2.cloned.1.call-done = bf16[512,4096]{1,0:T(8,128)(2,1)} async-done(((bf16[512,256]{1,0:T(8,128)(2,1)}), bf16[512,4096]{1,0:T(8,128)(2,1)}) %all-gather.2.cloned.1.call-update) | async-done | bytes 4194320 | tf_op jit(solution)/shard_map/all_gather | solution.py:85
  89.4 3.5 %fusion = bf16[256,4096]{1,0:T(8,128)(2,1)S(1)} fusion(bf16[512,256]{1,0:T(8,128)(2,1)S(1)} %reshape.35, bf16[512,4096]{1,0:T(8,128)(2,1)} %all-gather.2.cloned.1.call-done), kind=kOutput, calls=%fused_computation.1 | convolution fusion | flops 1075838976 | bytes 6553600 | tf_op jit(solution)/shard_map/dot_general | solution.py:49
  92.9 8.0 %convert_element_type.41 = bf16[8,32,128,32]{3,2,1,0:T(8,128)(2,1)} reshape(bf16[256,4096]{1,0:T(8,128)(2,1)S(1)} %fusion) | data formatting | bytes 4194304 | tf_op jit(solution)/shard_map/convert_element_type | solution.py:53
  100.9 0.0 copy-start.5
  100.9 7.0 %copy.11 = bf16[8,128,32,32]{1,0,3,2:T(8,128)(2,1)S(1)} copy(bf16[8,128,32,32]{3,1,2,0:T(8,128)(2,1)} %bitcast.26) | data formatting | bytes 4194304 | tf_op jit(solution)/shard_map/convert_element_type | solution.py:53
  107.9 0.0 copy-done
  107.9 0.0 copy-done.5
  107.9 1.5 %fusion.7 = bf16[1024,128]{1,0:T(8,128)(2,1)} fusion(bf16[1024,128]{1,0:T(8,128)(2,1)S(1)} %copy-done, bf16[128,8,8,128]{3,2,1,0:T(8,128)(2,1)S(1)} %bitcast.27, f32[128]{0:T(128)S(1)} %copy-done.5), kind=kOutput, calls=%fused_computation.10 | convolution fusion | flops 268697600 | bytes 2621952 | tf_op jit(solution)/shard_map/dot_general | solution.py:54
  (2 shorter events, 0.0 us)
Async XLA Ops:
  6.5 101.3 %copy-start = (bf16[1024,128]{1,0:T(8,128)(2,1)S(1)}, bf16[1024,128]{1,0:T(8,128)(2,1)}, u32[]{:S(2)}) copy-start(bf16[1024,128]{1,0:T(8,128)(2,1)} %param.12) | copy-start | bytes 786436
  6.5 82.8 %all-gather.2.cloned.1.call-start = ((), (), s32[]{:S(2)}) async-start(), calls=%async_computation.1 | async-start | bytes 4456448 | tf_op jit(solution)/shard_map/all_gather | solution.py:85
  29.9 2.0 %copy-start.3 = (f32[64]{0:T(128)S(1)}, f32[64]{0:T(128)}, u32[]{:S(2)}) copy-start(f32[64]{0:T(128)} %param.9) | copy-start | bytes 772
  29.9 2.0 %copy-start.4 = (f32[64]{0:T(128)S(1)}, f32[64]{0:T(128)}, u32[]{:S(2)}) copy-start(f32[64]{0:T(128)} %param.8) | copy-start | bytes 772
  31.8 2.4 %copy-start.1 = (bf16[64,32]{0,1:T(8,128)(2,1)S(1)}, bf16[64,32]{0,1:T(8,128)(2,1)}, u32[]{:S(2)}) copy-start(bf16[64,32]{0,1:T(8,128)(2,1)} %param.11) | copy-start | bytes 12292
  34.2 2.4 %copy-start.2 = (bf16[64,32]{0,1:T(8,128)(2,1)S(1)}, bf16[64,32]{0,1:T(8,128)(2,1)}, u32[]{:S(2)}) copy-start(bf16[64,32]{0,1:T(8,128)(2,1)} %param.10) | copy-start | bytes 12292
  100.9 7.0 %copy-start.5 = (f32[128]{0:T(128)S(1)}, f32[128]{0:T(128)}, u32[]{:S(2)}) copy-start(f32[128]{0:T(128)} %param.13) | copy-start | bytes 1540
Sparse Core Ops, SparseCore 0:
  36.7 52.6 all-gather.1
where the time goes:
time: 117 us; the launch traced here: 116 us
  waiting for transfers between devices  51.1 us (44%)
  blocking collectives  21.7 us (19%)
  local copies, waits for them, and re-layouts  19.7 us (17%)
  between operations  13.6 us (12%)
  matrix products  5.84 us (5%)
  other arithmetic  4.31 us (4%)
    all_gather x1, waiting for transfers between devices, on_device(): lax.all_gather(right, 'res', axis=1, tiled=True)  51.1 us
    all_to_all x1, blocking collectives, on_device(): lax.all_to_all(stacked_sequence_embedding, 'res', split_axis=1, concat_ax...  21.7 us
    convert_element_type x2, local copies, waits for them, and re-layouts, pair_block(): flat.reshape(left_count * right_count, width * width).astype(jnp.bfloat16)  15 us
    dot_general x1, matrix products, pair_block(): lax.dot_general(left, piece, (((0,), (0,)), ((), ())), preferred_element_...  3.47 us
  transfers between devices with their start and end apart: 1, of which 1 were waited for; matrix products, arithmetic and copies ran while one was open for 1% of the time, Pallas kernels for 0%

commit v1 on v0

--- a/solution.py
+++ b/solution.py
@@ -66,8 +66,14 @@
 ):
     chans = lhs_projected_tensor.shape[0]
     width = lhs_projected_tensor.shape[1]
-    partition_numbers = lax.all_to_all(
-        stacked_sequence_embedding, "res", split_axis=1, concat_axis=0, tiled=True
+    partition_numbers = jnp.concatenate(
+        lax.all_to_all(
+            jnp.stack(jnp.split(stacked_sequence_embedding, lax.axis_size("res"), axis=1)),
+            "res",
+            0,
+            0,
+        ),
+        axis=0,
     )
     rows = partition_numbers.shape[0]
     resid = partition_numbers.shape[1] // chans

time: 117 us -> 128 us (1.094)
  local copies, waits for them, and re-layouts: 19.7 us -> 30.8 us
    unnamed x12 -> x27, local copies, waits for them, and re-layouts: 0.03 us -> 11.5 us
where the time goes in v1:
time: 128 us; the launch traced here: 127 us
  waiting for transfers between devices  51.1 us (40%)
  local copies, waits for them, and re-layouts  30.8 us (24%)
  blocking collectives  21.6 us (17%)
  between operations  13.6 us (11%)
  matrix products  5.84 us (5%)
  other arithmetic  4.2 us (3%)
    all_gather x1, waiting for transfers between devices, on_device(): lax.all_gather(right, 'res', axis=1, tiled=True)  51.1 us
    all_to_all x1, blocking collectives, on_device(): lax.all_to_all(jnp.stack(jnp.split(stacked_sequence_embedding, lax.axis_s...  21.6 us
    convert_element_type x2, local copies, waits for them, and re-layouts, pair_block(): flat.reshape(left_count * right_count, width * width).astype(jnp.bfloat16)  15 us
    unnamed x27, local copies, waits for them, and re-layouts  11.5 us
    dot_general x1, matrix products, pair_block(): lax.dot_general(left, piece, (((0,), (0,)), ((), ())), preferred_element_...  3.47 us
  transfers between devices with their start and end apart: 1, of which 1 were waited for; matrix products, arithmetic and copies ran while one was open for 1% of the time, Pallas kernels for 0%

profile of v1, /device:TPU:0, one launch (start us, length us, event | category | flops | bytes accessed | tf_op | source)
XLA Modules:
  0.0 127.2 jit_solution(2069086437250552977)
XLA Ops:
  6.5 0.8 constant_dynamic-update-slice_fusion.15
  7.3 0.8 constant_dynamic-update-slice_fusion.14
  8.1 0.8 constant_dynamic-update-slice_fusion.13
  8.9 0.8 constant_dynamic-update-slice_fusion.12
  9.6 0.8 constant_dynamic-update-slice_fusion.11
  10.4 0.8 constant_dynamic-update-slice_fusion.10
  11.1 0.8 constant_dynamic-update-slice_fusion.9
  11.9 0.8 constant_dynamic-update-slice_fusion.8
  12.7 0.8 constant_dynamic-update-slice_fusion.7
  13.4 0.8 constant_dynamic-update-slice_fusion.6
  14.2 0.8 constant_dynamic-update-slice_fusion.5
  14.9 0.8 constant_dynamic-update-slice_fusion.4
  15.7 0.8 constant_dynamic-update-slice_fusion.3
  16.5 0.8 constant_dynamic-update-slice_fusion.2
  17.2 0.8 constant_dynamic-update-slice_fusion.1
  18.0 0.8 constant_dynamic-update-slice_fusion
  18.8 21.6 %all_to_all.5 = bf16[16,32,512]{2,1,0:T(8,128)(2,1)S(1)} all-to-all(bf16[16,32,512]{2,1,0:T(8,128)(2,1)S(1)} %constant_dynamic-update-slice_fusion), channel_id=1, replica_groups=mesh['grp'=2,'res'=16] {'res'}, dimensions={0} | all-to-all | bytes 1048576 | tf_op jit(solution)/shard_map/all_to_all | solution.py:70
  40.4 0.4 reshape.36
  40.8 0.6 reduce_sum.18
  41.5 1.3 %multiply_reduce_fusion = f32[4096]{0:T(1024)S(1)} fusion(f32[4096,64]{1,0:T(8,128)S(1)} %reshape.36, f32[4096]{0:T(1024)S(1)} %broadcast_multiply_fusion), kind=kLoop, calls=%fused_computation.8 | loop fusion | flops 782336 | bytes 1081344 | tf_op jit(solution)/shard_map/reduce_sum | solution.py:9
  42.8 2.3 %add_convert_fusion = bf16[4096,64]{1,0:T(8,128)(2,1)S(1)} fusion(f32[4096,64]{1,0:T(8,128)S(1)} %reshape.36, f32[64]{0:T(128)S(1)} %copy-done.3, f32[64]{0:T(128)S(1)} %copy-done.4, f32[4096]{0:T(1024)S(1)} %add_rsqrt_fusion, f32[4096]{0:T(1024)S(1)} %broadcast_multiply_fusion), kind=kLoop, calls=%fused_computation.7 | loop fusion | flops 1310720 | bytes 1606144 | tf_op jit(solution)/shard_map/convert_element_type | solution.py:12
  45.1 0.4 convolution_convert_fusion
  45.6 0.5 copy.9
  46.1 1.4 %reshape.34 = bf16[512,256]{1,0:T(8,128)(2,1)} reshape(bf16[4096,32]{1,0:T(8,128)(2,1)S(1)} %copy.9) | data formatting | bytes 524288 | tf_op jit(solution)/shard_map/reshape | solution.py:39
  47.5 0.4 convolution_convert_fusion.1
  48.0 0.5 copy.8
  48.5 0.7 reshape.33
  49.2 51.1 %all-gather.2.cloned.1.call-done = bf16[512,4096]{1,0:T(8,128)(2,1)} async-done(((bf16[512,256]{1,0:T(8,128)(2,1)}), bf16[512,4096]{1,0:T(8,128)(2,1)}) %all-gather.2.cloned.1.call-update) | async-done | bytes 4194320 | tf_op jit(solution)/shard_map/all_gather | solution.py:91
  100.3 3.5 %fusion = bf16[256,4096]{1,0:T(8,128)(2,1)S(1)} fusion(bf16[512,256]{1,0:T(8,128)(2,1)S(1)} %reshape.33, bf16[512,4096]{1,0:T(8,128)(2,1)} %all-gather.2.cloned.1.call-done), kind=kOutput, calls=%fused_computation.1 | convolution fusion | flops 1075838976 | bytes 6553600 | tf_op jit(solution)/shard_map/dot_general | solution.py:49
  103.8 8.0 %convert_element_type.37 = bf16[8,32,128,32]{3,2,1,0:T(8,128)(2,1)} reshape(bf16[256,4096]{1,0:T(8,128)(2,1)S(1)} %fusion) | data formatting | bytes 4194304 | tf_op jit(solution)/shard_map/convert_element_type | solution.py:53
  111.8 7.0 %copy.10 = bf16[8,128,32,32]{1,0,3,2:T(8,128)(2,1)S(1)} copy(bf16[8,128,32,32]{3,1,2,0:T(8,128)(2,1)} %bitcast.52) | data formatting | bytes 4194304 | tf_op jit(solution)/shard_map/convert_element_type | solution.py:53
  118.8 1.5 %fusion.7 = bf16[1024,128]{1,0:T(8,128)(2,1)} fusion(bf16[1024,128]{1,0:T(8,128)(2,1)S(1)} %copy-done, bf16[128,8,8,128]{3,2,1,0:T(8,128)(2,1)S(1)} %bitcast.53, f32[128]{0:T(128)S(1)} %copy-done.5), kind=kOutput, calls=%fused_computation.10 | convolution fusion | flops 268697600 | bytes 2621952 | tf_op jit(solution)/shard_map/dot_general | solution.py:54
  (16 shorter events, 0.1 us)
Async XLA Ops:
  6.5 112.3 %copy-start = (bf16[1024,128]{1,0:T(8,128)(2,1)S(1)}, bf16[1024,128]{1,0:T(8,128)(2,1)}, u32[]{:S(2)}) copy-start(bf16[1024,128]{1,0:T(8,128)(2,1)} %param.12) | copy-start | bytes 786436
  6.5 93.8 %all-gather.2.cloned.1.call-start = ((), (), s32[]{:S(2)}) async-start(), calls=%async_computation.1 | async-start | bytes 4456448 | tf_op jit(solution)/shard_map/all_gather | solution.py:91
  40.8 2.0 %copy-start.3 = (f32[64]{0:T(128)S(1)}, f32[64]{0:T(128)}, u32[]{:S(2)}) copy-start(f32[64]{0:T(128)} %param.9) | copy-start | bytes 772
  40.8 2.0 %copy-start.4 = (f32[64]{0:T(128)S(1)}, f32[64]{0:T(128)}, u32[]{:S(2)}) copy-start(f32[64]{0:T(128)} %param.8) | copy-start | bytes 772
  42.8 2.4 %copy-start.1 = (bf16[64,32]{0,1:T(8,128)(2,1)S(1)}, bf16[64,32]{0,1:T(8,128)(2,1)}, u32[]{:S(2)}) copy-start(bf16[64,32]{0,1:T(8,128)(2,1)} %param.11) | copy-start | bytes 12292
  45.1 2.4 %copy-start.2 = (bf16[64,32]{0,1:T(8,128)(2,1)S(1)}, bf16[64,32]{0,1:T(8,128)(2,1)}, u32[]{:S(2)}) copy-start(bf16[64,32]{0,1:T(8,128)(2,1)} %param.10) | copy-start | bytes 12292
  111.8 7.0 %copy-start.5 = (f32[128]{0:T(128)S(1)}, f32[128]{0:T(128)}, u32[]{:S(2)}) copy-start(f32[128]{0:T(128)} %param.13) | copy-start | bytes 1540
Sparse Core Ops, SparseCore 0:
  47.7 52.6 all-gather.1
